TPU v7x, 256 devices: a whole 4x4x8 slice. The times are simulated.
256 devices in a mesh: dp: 32 (over y, z_lo, core), seq: 8 (over z_hi, x).
Axes of the slice: x: 4, y: 4, z: 8 (z_hi: 2, z_lo: 4; z = z_hi * 4 + z_lo), core: 2. Of those that a mesh axis runs over, the one named last changes fastest.
Arguments:
- query: bfloat16 [36864, 2048], P(('dp', 'seq')), may hold values from -32 to 32
- key_in: bfloat16 [36864, 2048], P(('dp', 'seq')), may hold values from -6.5 to 6.5
- value: bfloat16 [36864, 2048], P(('dp', 'seq')), may hold values from -6 to 6
- out_weight: bfloat16 [2048, 3072], P('dp'), may hold values from -0.125 to 0.125
- out_grad: bfloat16 [36864, 3072], P(('dp', 'seq')), may hold values from -6 to 6
- windows: int32 [96, 5], P('dp'), may hold values from 0 to 95, as said below
- window_count: int32 [96], P('dp'), may hold values from 1 to 5, as said below
Outputs:
- output: bfloat16 [36864, 3072], P(('dp', 'seq'))
- d_query: bfloat16 [36864, 2048], P(('dp', 'seq'))
- d_key: bfloat16 [36864, 2048], P(('dp', 'seq'))
- d_value: bfloat16 [36864, 2048], P(('dp', 'seq'))
Inputs may be any that keep to these rules, and one draw needn't show every extreme that they name: `windows`: row t names 5 different tiles; its first entry is t itself, and every entry lies in tile t's slab or in the slab just before or after it, a slab being 3 consecutive tiles. Tile t attends to the first window_count[t] tiles of its row; some tile attends to all 5 and some to one.
All inputs are finite; a program needn't handle non-finite values.
Results may differ from a plain program's by a relative error of at most 0.0075.
Values may be sent and summed in bfloat16 or wider, within the bound.
A program may use at most 192 MiB of HBM per device.

v0:
```python
import jax
import jax.numpy as jnp
from jax import lax
from jax.sharding import PartitionSpec as P

HD = 128
TILE = 384


def extended_2(block, sides, width):
    for axis, dim in sides:
        count = lax.axis_size(axis)
        forward = [(i, i + 1) for i in range(count - 1)]
        backward = [(target, source) for source, target in forward]
        low = lax.ppermute(
            lax.slice_in_dim(block, block.shape[dim] - width, None, axis=dim), axis, forward
        )
        high = lax.ppermute(lax.slice_in_dim(block, 0, width, axis=dim), axis, backward)
        block = jnp.concatenate([low, block, high], axis=dim)
    return block


def make_fold(source, out_grad, portion):
    out_sum = jnp.dot(source, portion, preferred_element_type=jnp.float32)
    product = jnp.einsum("td,rd->tr", out_grad, portion, preferred_element_type=jnp.float32).astype(
        jnp.bfloat16
    )
    return (out_sum, product)


def body(query, key_in, value, out_weight, out_grad, windows, window_count):
    tile_count = windows.shape[0]
    window = windows.shape[1]
    factor = HD ** (-0.5)
    q_heads, k_heads, v_heads = (
        lax.all_to_all(query, "seq", split_axis=1, concat_axis=0, tiled=True),
        lax.all_to_all(key_in, "seq", split_axis=1, concat_axis=0, tiled=True),
        lax.all_to_all(value, "seq", split_axis=1, concat_axis=0, tiled=True),
    )
    slab_rows = q_heads.shape[0]
    width_local = q_heads.shape[1]
    head_count = width_local // HD
    stacked = jnp.concatenate([k_heads, v_heads], axis=1)
    extended = extended_2(stacked, (("dp", 0),), slab_rows)
    blocks = extended.reshape(3 * tile_count, TILE, 2, head_count, HD)
    lowest = (lax.axis_index("dp") - 1) * tile_count
    local_ids = windows - lowest
    query_tiles = q_heads.reshape(tile_count, TILE, head_count, HD)

    def forward_tile(members):
        query_tile, tile_ids, filled = members
        gathered = blocks[tile_ids]
        keyed_rows = gathered[:, :, 0]
        value_rows = gathered[:, :, 1]
        scores = (
            jnp.einsum("qhd,wkhd->hqwk", query_tile, keyed_rows, preferred_element_type=jnp.float32)
            * factor
        )
        allowed = (jnp.arange(window) < filled)[None, None, :, None]
        scores = jnp.where(allowed, scores, -jnp.inf)
        largest = jnp.max(scores, axis=(2, 3), keepdims=True)
        raised = jnp.exp(scores - largest)
        total = jnp.sum(raised, axis=(2, 3), keepdims=True)
        weights = raised / total
        attn_tile = jnp.einsum(
            "hqwk,wkhd->qhd",
            weights.astype(jnp.bfloat16),
            value_rows,
            preferred_element_type=jnp.float32,
        ).astype(jnp.bfloat16)
        return (attn_tile, weights, largest[:, :, 0, 0], total[:, :, 0, 0])

    attn_tiles, saved_weights, saved_largest, saved_total = lax.map(
        forward_tile, (query_tiles, local_ids, window_count)
    )
    attn_heads = attn_tiles.reshape(slab_rows, width_local)
    attn_tokens = lax.all_to_all(attn_heads, "seq", split_axis=0, concat_axis=1, tiled=True)
    out_sum, grad_tokens = make_fold(
        attn_tokens, out_grad, lax.all_gather(out_weight, "dp", axis=0, tiled=True)
    )
    output = out_sum.astype(jnp.bfloat16)
    grad_heads = lax.all_to_all(grad_tokens, "seq", split_axis=1, concat_axis=0, tiled=True)
    grad_tiles = grad_heads.reshape(tile_count, TILE, head_count, HD)

    def backward_tile(members):
        query_tile, tile_ids, weights, grad_tile = members
        gathered = blocks[tile_ids]
        keyed_rows = gathered[:, :, 0]
        value_rows = gathered[:, :, 1]
        rounded = weights.astype(jnp.bfloat16)
        grad_weights = jnp.einsum(
            "qhd,wkhd->hqwk", grad_tile, value_rows, preferred_element_type=jnp.float32
        )
        centre = jnp.sum(weights * grad_weights, axis=(2, 3), keepdims=True)
        grad_scores = (weights * (grad_weights - centre) * factor).astype(jnp.bfloat16)
        grad_query = jnp.einsum(
            "hqwk,wkhd->qhd", grad_scores, keyed_rows, preferred_element_type=jnp.float32
        ).astype(jnp.bfloat16)
        grad_keyed = jnp.einsum(
            "hqwk,qhd->wkhd", grad_scores, query_tile, preferred_element_type=jnp.float32
        )
        grad_valued = jnp.einsum(
            "hqwk,qhd->wkhd", rounded, grad_tile, preferred_element_type=jnp.float32
        )
        return (grad_query, grad_keyed, grad_valued, centre[:, :, 0, 0])

    query_grads, keyed_parts, valued_parts, saved_centre = lax.map(
        backward_tile, (query_tiles, local_ids, saved_weights, grad_tiles)
    )
    flat_size = TILE * width_local
    onehot = (local_ids.reshape(-1)[:, None] == jnp.arange(3 * tile_count)[None, :]).astype(
        jnp.float32
    )
    keyed_ext = jnp.einsum(
        "ns,nx->sx",
        onehot,
        keyed_parts.reshape(tile_count * window, flat_size),
        precision=lax.Precision.HIGHEST,
    ).reshape(3 * slab_rows, width_local)
    valued_ext = jnp.einsum(
        "ns,nx->sx",
        onehot,
        valued_parts.reshape(tile_count * window, flat_size),
        precision=lax.Precision.HIGHEST,
    ).reshape(3 * slab_rows, width_local)
    combined = jnp.concatenate([keyed_ext, valued_ext], axis=1)
    outer_rims = jnp.concatenate([combined[:slab_rows], combined[2 * slab_rows :]], axis=0)
    arrived = extended_2(outer_rims.astype(jnp.bfloat16), (("dp", 0),), slab_rows).astype(
        outer_rims.dtype
    )
    summed = combined[slab_rows : 2 * slab_rows] + arrived[:slab_rows] + arrived[3 * slab_rows :]
    key_heads = summed[:, :width_local].astype(jnp.bfloat16)
    value_heads = summed[:, width_local:].astype(jnp.bfloat16)
    query_heads = query_grads.reshape(slab_rows, width_local)
    d_query, d_key, d_value = (
        lax.all_to_all(query_heads, "seq", split_axis=0, concat_axis=1, tiled=True),
        lax.all_to_all(key_heads, "seq", split_axis=0, concat_axis=1, tiled=True),
        lax.all_to_all(value_heads, "seq", split_axis=0, concat_axis=1, tiled=True),
    )
    return (output, d_query, d_key, d_value)


def solution(mesh):
    in_specs = (
        P(("dp", "seq"), None),
        P(("dp", "seq"), None),
        P(("dp", "seq"), None),
        P("dp", None),
        P(("dp", "seq"), None),
        P("dp", None),
        P("dp"),
    )
    out_specs = (
        P(("dp", "seq"), None),
        P(("dp", "seq"), None),
        P(("dp", "seq"), None),
        P(("dp", "seq"), None),
    )
    return jax.shard_map(body, mesh=mesh, in_specs=in_specs, out_specs=out_specs, check_vma=False)
```

profile of v0, /device:TPU:32, one launch (start us, length us, event | category | flops | bytes accessed | tf_op | source)
XLA Modules:
  0.0 524.1 jit_solution(6442156912303026273)
XLA Ops:
  9.9 10.0 %all-to-all-start.1 = ((bf16[144,8,256]{2,0,1:T(8,128)(2,1)}), bf16[144,8,256]{2,0,1:T(8,128)(2,1)S(1)}, u32[]{:S(2)}, u32[]{:S(2)}) async-start(bf16[144,8,256]{2,0,1:T(8,128)(2,1)} %bitcast.149), calls=%async_computation.1 | async-start | bytes 1179648 | tf_op jit(solution)/shard_map/all_to_all | solution.py:38
  21.0 24.1 %all-to-all-done.1 = bf16[144,8,256]{2,0,1:T(8,128)(2,1)S(1)} async-done(((bf16[144,8,256]{2,0,1:T(8,128)(2,1)}), bf16[144,8,256]{2,0,1:T(8,128)(2,1)S(1)}, u32[]{:S(2)}, u32[]{:S(2)}) %all-to-all-start.1) | async-done | bytes 589856 | tf_op jit(solution)/shard_map/all_to_all | solution.py:38
  45.1 28.5 %all_to_all.146 = bf16[144,8,256]{2,0,1:T(8,128)(2,1)S(1)} all-to-all(bf16[144,8,256]{2,0,1:T(8,128)(2,1)S(1)} %bitcast.210), channel_id=1, replica_groups=mesh['dp'=32,'seq'=8] {'seq'}, dimensions={1} | all-to-all | bytes 1179648 | tf_op jit(solution)/shard_map/all_to_all | solution.py:37
  79.9 3.5 all-to-all-start.2
  84.1 64.2 %all-to-all-done.2 = bf16[144,8,256]{2,0,1:T(8,128)(2,1)S(1)} async-done(((bf16[144,8,256]{2,0,1:T(8,128)(2,1)}), bf16[144,8,256]{2,0,1:T(8,128)(2,1)S(1)}, u32[]{:S(2)}, u32[]{:S(2)}) %all-to-all-start.2) | async-done | bytes 589856 | tf_op jit(solution)/shard_map/all_to_all | solution.py:36
  148.4 3.6 pad_maximum_fusion
  152.0 8.4 %reshape.123 = bf16[9,384,2,2,128]{4,3,2,1,0:T(2,128)(2,1)} reshape(bf16[3456,512]{1,0:T(8,128)(2,1)} %pad_maximum_fusion) | data formatting | bytes 7077888 | tf_op jit(solution)/shard_map/reshape | solution.py:45
  160.4 4.6 copy.130
  164.9 8.9 %convolution_convert_fusion.1 = bf16[144,2048]{1,0:T(8,128)(2,1)S(1)} fusion(bf16[144,3072]{1,0:T(8,128)(2,1)S(1)} %copy-done, bf16[2048,3072]{1,0:T(8,128)(2,1)} %all-gather.2.cloned.1.call-done), kind=kOutput, calls=%fused_computation.55 | convolution fusion | flops 1812234240 | bytes 14057472 | tf_op jit(solution)/shard_map/td,rd->tr/dot_general | solution.py:25
  174.7 8.0 %all-to-all-start.4 = ((bf16[144,8,256]{2,0,1:T(8,128)(2,1)}), bf16[144,8,256]{2,0,1:T(8,128)(2,1)}, u32[]{:S(2)}, u32[]{:S(2)}) async-start(bf16[144,8,256]{2,0,1:T(8,128)(2,1)} %bitcast.147), calls=%async_computation.4 | async-start | bytes 1179648 | tf_op jit(solution)/shard_map/all_to_all | solution.py:82
  183.8 64.0 %while.26 = (s32[]{:T(128)}, bf16[3,384,2,128]{3,2,1,0:T(2,128)(2,1)}, f32[3,2,384,5,384]{2,4,3,1,0:T(8,128)}, s32[3,5]{1,0:T(4,128)S(1)}, bf16[9,384,2,2,128]{4...) while((s32[]{:T(128)}, bf16[3,384,2,128]{3,2,1,0:T(2,128)(2,1)}, ...), condition=%wide.region_3.4_spmd, body=%wide.region_0.3_spmd.sunk | while | flops 778665472 | bytes 66479360 | solution.py:73
  183.8 2.9 gather_fusion
  198.7 6.5 %bitcast_dynamic-update-slice_fusion.2 = f32[3,2,384,5,384]{2,4,3,1,0:T(8,128)} fusion(f32[3,2,384,5,384]{2,4,3,1,0:T(8,128)} %get-tuple-element.357, s32[]{:T(128)S(6)} %copy.236, f32[2,384]{1,0:T(2,128)S(1)} %fusion.72, f32[2,384]{1,0:T(2,128)S(1)} %get-tuple-element.331, f32[2,384,5,384]{1,3,2,0:T(8,128)} %copy-done.2, ...), kind=kLoop, calls=%fused_computation.2.clone.1 | loop fusion | flops 5898240 | bytes 11802633 | tf_op jit(solution)/shard_map/while/body/jit(dynamic_update_index_in_dim)/dynamic_update_slice | solution.py:73
  220.1 6.4 %bitcast_dynamic-update-slice_fusion.2 = f32[3,2,384,5,384]{2,4,3,1,0:T(8,128)} fusion(f32[3,2,384,5,384]{2,4,3,1,0:T(8,128)} %get-tuple-element.357, s32[]{:T(128)S(6)} %copy.236, f32[2,384]{1,0:T(2,128)S(1)} %fusion.72, f32[2,384]{1,0:T(2,128)S(1)} %get-tuple-element.331, f32[2,384,5,384]{1,3,2,0:T(8,128)} %copy-done.2, ...), kind=kLoop, calls=%fused_computation.2.clone.1 | loop fusion | flops 5898240 | bytes 11802633 | tf_op jit(solution)/shard_map/while/body/jit(dynamic_update_index_in_dim)/dynamic_update_slice | solution.py:73
  241.4 6.4 %bitcast_dynamic-update-slice_fusion.2 = f32[3,2,384,5,384]{2,4,3,1,0:T(8,128)} fusion(f32[3,2,384,5,384]{2,4,3,1,0:T(8,128)} %get-tuple-element.357, s32[]{:T(128)S(6)} %copy.236, f32[2,384]{1,0:T(2,128)S(1)} %fusion.72, f32[2,384]{1,0:T(2,128)S(1)} %get-tuple-element.331, f32[2,384,5,384]{1,3,2,0:T(8,128)} %copy-done.2, ...), kind=kLoop, calls=%fused_computation.2.clone.1 | loop fusion | flops 5898240 | bytes 11802633 | tf_op jit(solution)/shard_map/while/body/jit(dynamic_update_index_in_dim)/dynamic_update_slice | solution.py:73
  250.7 104.2 %while.27 = (s32[]{:T(128)}, bf16[3,384,2,128]{3,2,1,0:T(2,128)(2,1)}, f32[3,5,384,2,128]{4,3,2,1,0:T(2,128)}, f32[3,5,384,2,128]{4,3,2,1,0:T(2,128)}, s32[3,5]{...) while((s32[]{:T(128)}, ...), condition=%wide.region_6.7_spmd, body=%wide.region_4.6_spmd.sunk | while | flops 1518895360 | bytes 78260528 | solution.py:107
  250.9 3.1 gather_fusion.1
  255.3 3.7 fusion.80
  259.0 5.4 %fusion.81 = bf16[2,384,5,384]{1,3,2,0:T(8,128)(2,1)} fusion(f32[2,384,5,384]{1,3,2,0:T(8,128)S(1)} %get-tuple-element.342, f32[3,2,384,5,384]{2,4,3,1,0:T(8,128)} %get-tuple-element.397, s32[]{:T(128)S(6)} %copy.246, f32[2,384]{1,0:T(2,128)S(1)} %get-tuple-element.343), kind=kLoop, calls=%fused_computation.30.clone.1 | loop fusion | flops 5898240 | bytes 14748676 | tf_op jit(solution)/shard_map/while/body/eval_jaxpr/convert_element_type | solution.py:95
  268.6 3.7 fusion.83
  281.2 4.3 constant_dynamic-update-slice_fusion.11
  285.6 3.1 gather_fusion.1
  289.9 3.7 fusion.80
  293.6 5.4 %fusion.81 = bf16[2,384,5,384]{1,3,2,0:T(8,128)(2,1)} fusion(f32[2,384,5,384]{1,3,2,0:T(8,128)S(1)} %get-tuple-element.342, f32[3,2,384,5,384]{2,4,3,1,0:T(8,128)} %get-tuple-element.397, s32[]{:T(128)S(6)} %copy.246, f32[2,384]{1,0:T(2,128)S(1)} %get-tuple-element.343), kind=kLoop, calls=%fused_computation.30.clone.1 | loop fusion | flops 5898240 | bytes 14748676 | tf_op jit(solution)/shard_map/while/body/eval_jaxpr/convert_element_type | solution.py:95
  303.2 3.7 fusion.83
  315.9 4.4 constant_dynamic-update-slice_fusion.11
  320.3 3.1 gather_fusion.1
  324.6 3.7 fusion.80
  328.3 5.4 %fusion.81 = bf16[2,384,5,384]{1,3,2,0:T(8,128)(2,1)} fusion(f32[2,384,5,384]{1,3,2,0:T(8,128)S(1)} %get-tuple-element.342, f32[3,2,384,5,384]{2,4,3,1,0:T(8,128)} %get-tuple-element.397, s32[]{:T(128)S(6)} %copy.246, f32[2,384]{1,0:T(2,128)S(1)} %get-tuple-element.343), kind=kLoop, calls=%fused_computation.30.clone.1 | loop fusion | flops 5898240 | bytes 14748676 | tf_op jit(solution)/shard_map/while/body/eval_jaxpr/convert_element_type | solution.py:95
  337.9 3.7 fusion.83
  350.6 4.3 constant_dynamic-update-slice_fusion.11
  354.9 8.6 %reshape.126 = f32[15,98304]{1,0:T(8,128)} reshape(f32[3,5,384,2,128]{4,3,2,1,0:T(2,128)} %get-tuple-element.94) | data formatting | bytes 11796480 | tf_op jit(solution)/shard_map/reshape | solution.py:117
  363.5 8.1 %fusion.35 = f32[9,98304]{1,0:T(8,128)} fusion(f32[15,98304]{1,0:T(8,128)} %reshape.126, s32[15]{0:T(128)S(1)} %copy-done.8), kind=kOutput, calls=%fused_computation.69 | convolution fusion | flops 159252608 | bytes 9437244 | tf_op jit(solution)/shard_map/ns,nx->sx/dot_general | solution.py:114
  371.6 4.3 reshape.127
  375.9 4.2 constant_dynamic-update-slice_fusion.5
  380.1 8.5 %reshape.128 = f32[15,98304]{1,0:T(8,128)} reshape(f32[3,5,384,2,128]{4,3,2,1,0:T(2,128)} %get-tuple-element.95) | data formatting | bytes 11796480 | tf_op jit(solution)/shard_map/reshape | solution.py:123
  388.6 8.1 %fusion.34 = f32[9,98304]{1,0:T(8,128)} fusion(f32[15,98304]{1,0:T(8,128)} %reshape.128, s32[15]{0:T(128)S(1)} %copy-done.8), kind=kOutput, calls=%fused_computation.68 | convolution fusion | flops 159252608 | bytes 9437244 | tf_op jit(solution)/shard_map/ns,nx->sx/dot_general | solution.py:120
  396.7 4.1 reshape.129
  400.8 4.1 constant_dynamic-update-slice_fusion.4
  404.9 3.5 convert.10
  414.1 9.6 %all-to-all-start.3 = ((bf16[8,144,256]{2,1,0:T(8,128)(2,1)}), bf16[8,144,256]{2,1,0:T(8,128)(2,1)S(1)}, u32[]{:S(2)}, u32[]{:S(2)}) async-start(bf16[8,144,256]{2,1,0:T(8,128)(2,1)} %all_to_all.119), calls=%async_computation.3 | async-start | bytes 1179648 | tf_op jit(solution)/shard_map/all_to_all | solution.py:77
  426.5 32.6 %all-to-all-done.3 = bf16[8,144,256]{2,1,0:T(8,128)(2,1)S(1)} async-done(((bf16[8,144,256]{2,1,0:T(8,128)(2,1)}), bf16[8,144,256]{2,1,0:T(8,128)(2,1)S(1)}, u32[]{:S(2)}, u32[]{:S(2)}) %all-to-all-start.3) | async-done | bytes 589856 | tf_op jit(solution)/shard_map/all_to_all | solution.py:77
  459.1 4.2 all-to-all-start.5
  463.4 6.8 %fusion.33 = bf16[1152,512]{1,0:T(8,128)(2,1)S(1)} fusion(f32[3456,512]{1,0:T(8,128)} %constant_dynamic-update-slice_fusion.4, bf16[1152,512]{1,0:T(8,128)(2,1)} %collective-permute-done.3, bf16[1152,512]{1,0:T(8,128)(2,1)S(1)} %get-tuple-element.225, bf16[1152,512]{1,0:T(8,128)(2,1)S(1)} %get-tuple-element.226, bf16[1152,512]{1,0:T(8,128)(2,1)} %collective-permute-done.2), kind=kLoop, calls=%fused_computation.58 | loop fusion | flops 11206656 | bytes 8257536 | tf_op jit(solution)/shard_map/convert.1
  471.0 8.0 %all-to-all-done.5 = bf16[8,144,256]{2,1,0:T(8,128)(2,1)} async-done(((bf16[8,144,256]{2,1,0:T(8,128)(2,1)}), bf16[8,144,256]{2,1,0:T(8,128)(2,1)}, u32[]{:S(2)}, u32[]{:S(2)}) %all-to-all-start.5) | async-done | bytes 589856 | tf_op jit(solution)/shard_map/all_to_all | solution.py:136
  479.0 21.2 %all_to_all.147 = bf16[8,144,256]{2,1,0:T(8,128)(2,1)S(1)} all-to-all(bf16[8,144,256]{2,1,0:T(8,128)(2,1)S(1)} %bitcast.211), channel_id=1, replica_groups=mesh['dp'=32,'seq'=8] {'seq'}, dimensions={0} | all-to-all | bytes 1179648 | tf_op jit(solution)/shard_map/all_to_all | solution.py:137
  500.2 3.5 all-to-all-start.7
  503.8 7.6 %convolution_convert_fusion = bf16[144,3072]{1,0:T(8,128)(2,1)} fusion(bf16[144,2048]{1,0:T(8,128)(2,1)S(1)} %bitcast.205, bf16[2048,3072]{1,0:T(8,128)(2,1)} %all-gather.2.cloned.1.call-done), kind=kOutput, calls=%fused_computation.53 | convolution fusion | flops 1812381696 | bytes 14057472 | tf_op jit(solution)/shard_map/dot_general | solution.py:24
  (150 shorter events, 115.2 us)
Async XLA Ops:
  7.2 157.8 %copy-start = (bf16[144,3072]{1,0:T(8,128)(2,1)S(1)}, bf16[144,3072]{1,0:T(8,128)(2,1)}, u32[]{:S(2)}) copy-start(bf16[144,3072]{1,0:T(8,128)(2,1)} %param.15) | copy-start | bytes 2654212
  7.2 71.8 %copy-start.7 = (bf16[144,2048]{1,0:T(8,128)(2,1)S(1)}, bf16[144,2048]{1,0:T(8,128)(2,1)}, u32[]{:S(2)}) copy-start(bf16[144,2048]{1,0:T(8,128)(2,1)} %param.11) | copy-start | bytes 1769476
  7.2 76.3 %copy-start.9 = (s32[3,5]{1,0:T(4,128)S(1)}, s32[3,5]{1,0:T(4,128)}, u32[]{:S(2)}) copy-start(s32[3,5]{1,0:T(4,128)} %param.16) | copy-start | bytes 184
  7.2 157.7 %all-gather.2.cloned.1.call-start = ((), (), s32[]{:S(2)}) async-start(), calls=%async_computation.8 | async-start | bytes 12976128 | tf_op jit(solution)/shard_map/all_gather | solution.py:79
  9.9 35.2 %all-to-all-start.1 = ((bf16[144,8,256]{2,0,1:T(8,128)(2,1)}), bf16[144,8,256]{2,0,1:T(8,128)(2,1)S(1)}, u32[]{:S(2)}, u32[]{:S(2)}) async-start(bf16[144,8,256]{2,0,1:T(8,128)(2,1)} %bitcast.149), calls=%async_computation.1 | async-start | bytes 1179648 | tf_op jit(solution)/shard_map/all_to_all | solution.py:38
  74.7 73.8 %collective-permute-start.1 = (bf16[1152,512]{1,0:T(8,128)(2,1)}, bf16[1152,512]{1,0:T(8,128)(2,1)}, u32[]{:S(2)}, u32[]{:S(2)}) collective-permute-start(bf16[1152,512]{1,0:T(8,128)(2,1)} %pad_maximum_fusion.4), channel_id=1, source_target_pairs={{8,0},{16,8},{24,16},{32,24},{40,32},{48,40},{56,48},{64,56},{72,6... | collective-permute-start | bytes 3538952 | tf_op jit(solution)/shard_map/ppermute | solution.py:18
  76.6 71.9 %collective-permute-start = (bf16[1152,512]{1,0:T(8,128)(2,1)}, bf16[1152,512]{1,0:T(8,128)(2,1)}, u32[]{:S(2)}, u32[]{:S(2)}) collective-permute-start(bf16[1152,512]{1,0:T(8,128)(2,1)} %pad_maximum_fusion.4), channel_id=1, source_target_pairs={{0,8},{8,16},{16,24},{24,32},{32,40},{40,48},{48,56},{56,64},{64,7... | collective-permute-start | bytes 3538952 | tf_op jit(solution)/shard_map/ppermute | solution.py:15
  79.9 68.4 %all-to-all-start.2 = ((bf16[144,8,256]{2,0,1:T(8,128)(2,1)}), bf16[144,8,256]{2,0,1:T(8,128)(2,1)S(1)}, u32[]{:S(2)}, u32[]{:S(2)}) async-start(bf16[144,8,256]{2,0,1:T(8,128)(2,1)} %bitcast.148), calls=%async_computation.2 | async-start | bytes 1179648 | tf_op jit(solution)/shard_map/all_to_all | solution.py:36
  164.9 18.8 %copy-start.10 = (s32[3]{0:T(128)S(1)}, s32[3]{0:T(128)}, u32[]{:S(2)}) copy-start(s32[3]{0:T(128)} %param.17) | copy-start | bytes 40
  174.7 73.1 %all-to-all-start.4 = ((bf16[144,8,256]{2,0,1:T(8,128)(2,1)}), bf16[144,8,256]{2,0,1:T(8,128)(2,1)}, u32[]{:S(2)}, u32[]{:S(2)}) async-start(bf16[144,8,256]{2,0,1:T(8,128)(2,1)} %bitcast.147), calls=%async_computation.4 | async-start | bytes 1179648 | tf_op jit(solution)/shard_map/all_to_all | solution.py:82
  193.4 2.5 copy-start.2
  214.9 2.5 copy-start.2
  236.1 2.5 copy-start.2
  250.9 8.1 %copy-start.4 = (bf16[3,384,2,128]{3,2,1,0:T(2,128)(2,1)}, bf16[3,384,2,128]{3,2,1,0:T(2,128)(2,1)S(1)}, u32[]{:S(2)}) copy-start(bf16[3,384,2,128]{3,2,1,0:T(2,128)(2,1)S(1)} %get-tuple-element.398) | copy-start | bytes 1769476 | tf_op jit(solution)/shard_map/while
  259.0 5.4 %copy-start.3 = (bf16[5,384,1,2,128]{4,1,3,2,0:T(8,128)(2,1)S(1)}, bf16[5,384,1,2,128]{4,1,3,2,0:T(8,128)(2,1)}, u32[]{:S(2)}) copy-start(bf16[5,384,1,2,128]{4,1,3,2,0:T(8,128)(2,1)} %get-tuple-element.344) | copy-start | bytes 2949124 | tf_op jit(solution)/shard_map/while
  278.3 7.2 %copy-start.5 = (bf16[3,384,2,128]{3,2,1,0:T(2,128)(2,1)S(1)}, bf16[3,384,2,128]{3,2,1,0:T(2,128)(2,1)}, u32[]{:S(2)}) copy-start(bf16[3,384,2,128]{3,2,1,0:T(2,128)(2,1)} %copy-done.4) | copy-start | bytes 1769476 | tf_op jit(solution)/shard_map/while
  285.5 8.1 %copy-start.4 = (bf16[3,384,2,128]{3,2,1,0:T(2,128)(2,1)}, bf16[3,384,2,128]{3,2,1,0:T(2,128)(2,1)S(1)}, u32[]{:S(2)}) copy-start(bf16[3,384,2,128]{3,2,1,0:T(2,128)(2,1)S(1)} %get-tuple-element.398) | copy-start | bytes 1769476 | tf_op jit(solution)/shard_map/while
  293.6 5.4 %copy-start.3 = (bf16[5,384,1,2,128]{4,1,3,2,0:T(8,128)(2,1)S(1)}, bf16[5,384,1,2,128]{4,1,3,2,0:T(8,128)(2,1)}, u32[]{:S(2)}) copy-start(bf16[5,384,1,2,128]{4,1,3,2,0:T(8,128)(2,1)} %get-tuple-element.344) | copy-start | bytes 2949124 | tf_op jit(solution)/shard_map/while
  313.0 7.3 %copy-start.5 = (bf16[3,384,2,128]{3,2,1,0:T(2,128)(2,1)S(1)}, bf16[3,384,2,128]{3,2,1,0:T(2,128)(2,1)}, u32[]{:S(2)}) copy-start(bf16[3,384,2,128]{3,2,1,0:T(2,128)(2,1)} %copy-done.4) | copy-start | bytes 1769476 | tf_op jit(solution)/shard_map/while
  320.2 8.1 %copy-start.4 = (bf16[3,384,2,128]{3,2,1,0:T(2,128)(2,1)}, bf16[3,384,2,128]{3,2,1,0:T(2,128)(2,1)S(1)}, u32[]{:S(2)}) copy-start(bf16[3,384,2,128]{3,2,1,0:T(2,128)(2,1)S(1)} %get-tuple-element.398) | copy-start | bytes 1769476 | tf_op jit(solution)/shard_map/while
  328.3 5.4 %copy-start.3 = (bf16[5,384,1,2,128]{4,1,3,2,0:T(8,128)(2,1)S(1)}, bf16[5,384,1,2,128]{4,1,3,2,0:T(8,128)(2,1)}, u32[]{:S(2)}) copy-start(bf16[5,384,1,2,128]{4,1,3,2,0:T(8,128)(2,1)} %get-tuple-element.344) | copy-start | bytes 2949124 | tf_op jit(solution)/shard_map/while
  347.6 7.3 %copy-start.5 = (bf16[3,384,2,128]{3,2,1,0:T(2,128)(2,1)S(1)}, bf16[3,384,2,128]{3,2,1,0:T(2,128)(2,1)}, u32[]{:S(2)}) copy-start(bf16[3,384,2,128]{3,2,1,0:T(2,128)(2,1)} %copy-done.4) | copy-start | bytes 1769476 | tf_op jit(solution)/shard_map/while
  354.9 8.6 %copy-start.8 = (s32[15]{0:T(128)S(1)}, s32[15]{0:T(128)}, u32[]{:S(2)}) copy-start(s32[15]{0:T(128)} %eq.15) | copy-start | bytes 184
  404.9 8.0 %copy-start.6 = (bf16[3,384,2,128]{3,2,1,0:T(2,128)(2,1)S(1)}, bf16[3,384,2,128]{3,2,1,0:T(2,128)(2,1)}, u32[]{:S(2)}) copy-start(bf16[3,384,2,128]{3,2,1,0:T(2,128)(2,1)} %get-tuple-element.91) | copy-start | bytes 1769476
  408.6 54.8 %collective-permute-start.3 = (bf16[1152,512]{1,0:T(8,128)(2,1)S(1)}, bf16[1152,512]{1,0:T(8,128)(2,1)}, u32[]{:S(2)}, u32[]{:S(2)}) collective-permute-start(bf16[1152,512]{1,0:T(8,128)(2,1)S(1)} %get-tuple-element.226), channel_id=1, source_target_pairs={{8,0},{16,8},{24,16},{32,24},{40,32},{48,40},{56,48},{64,56},{72,6... | collective-permute-start | bytes 3538952 | tf_op jit(solution)/shard_map/ppermute | solution.py:18
  410.5 52.8 %collective-permute-start.2 = (bf16[1152,512]{1,0:T(8,128)(2,1)S(1)}, bf16[1152,512]{1,0:T(8,128)(2,1)}, u32[]{:S(2)}, u32[]{:S(2)}) collective-permute-start(bf16[1152,512]{1,0:T(8,128)(2,1)S(1)} %get-tuple-element.225), channel_id=1, source_target_pairs={{0,8},{8,16},{16,24},{24,32},{32,40},{40,48},{48,56},{56,64},{64,7... | collective-permute-start | bytes 3538952 | tf_op jit(solution)/shard_map/ppermute | solution.py:15
  414.1 45.0 %all-to-all-start.3 = ((bf16[8,144,256]{2,1,0:T(8,128)(2,1)}), bf16[8,144,256]{2,1,0:T(8,128)(2,1)S(1)}, u32[]{:S(2)}, u32[]{:S(2)}) async-start(bf16[8,144,256]{2,1,0:T(8,128)(2,1)} %all_to_all.119), calls=%async_computation.3 | async-start | bytes 1179648 | tf_op jit(solution)/shard_map/all_to_all | solution.py:77
  459.1 19.9 %all-to-all-start.5 = ((bf16[8,144,256]{2,1,0:T(8,128)(2,1)}), bf16[8,144,256]{2,1,0:T(8,128)(2,1)}, u32[]{:S(2)}, u32[]{:S(2)}) async-start(bf16[8,144,256]{2,1,0:T(8,128)(2,1)} %all_to_all.126), calls=%async_computation.5 | async-start | bytes 1179648 | tf_op jit(solution)/shard_map/all_to_all | solution.py:136
  500.2 15.9 %all-to-all-start.7 = ((bf16[8,144,256]{2,1,0:T(8,128)(2,1)}), bf16[8,144,256]{2,1,0:T(8,128)(2,1)S(1)}, u32[]{:S(2)}, u32[]{:S(2)}) async-start(bf16[8,144,256]{2,1,0:T(8,128)(2,1)} %bitcast.43), calls=%async_computation.7 | async-start | bytes 1179648 | tf_op jit(solution)/shard_map/all_to_all | solution.py:138
  503.8 13.2 %copy-start.1 = (bf16[144,3072]{1,0:T(8,128)(2,1)S(1)}, bf16[144,3072]{1,0:T(8,128)(2,1)}, u32[]{:S(2)}) copy-start(bf16[144,3072]{1,0:T(8,128)(2,1)} %param.15) | copy-start | bytes 2654212
Sparse Core Ops, SparseCore 0:
  9.9 140.2 all-gather.1
where the time goes:
time: 532 us; the launch traced here: 524 us
  local copies, waits for them, and re-layouts  141 us (27%)
  waiting for transfers between devices  132 us (25%)
  matrix products  82.6 us (16%)
  other arithmetic  56.4 us (11%)
  blocking collectives  49.7 us (9%)
  starting transfers between devices  47.6 us (9%)
  between operations  14.5 us (3%)
    all_to_all x1, waiting for transfers between devices, body(): lax.all_to_all(query, 'seq', split_axis=1, concat_axis=0, tiled=True)  64.2 us
    all_to_all x1, waiting for transfers between devices, body(): lax.all_to_all(attn_heads, 'seq', split_axis=0, concat_axis=1, tiled=True)  32.6 us
    dynamic_update_slice x9, local copies, waits for them, and re-layouts, body(): lax.map(backward_tile, (query_tiles, local_ids, saved_weights, grad_tiles))  30.4 us
    all_to_all x1, blocking collectives, body(): lax.all_to_all(key_in, 'seq', split_axis=1, concat_axis=0, tiled=True)  28.5 us
    all_to_all x1, waiting for transfers between devices, body(): lax.all_to_all(value, 'seq', split_axis=1, concat_axis=0, tiled=True)  24.1 us
    all_to_all x1, blocking collectives, body(): lax.all_to_all(key_heads, 'seq', split_axis=0, concat_axis=1, tiled=True)  21.2 us
    dynamic_update_slice x3, other arithmetic, body(): lax.map(forward_tile, (query_tiles, local_ids, window_count))  19.3 us
    convert_element_type x3, other arithmetic, backward_tile(): (weights * (grad_weights - centre) * factor).astype(jnp.bfloat16)  16.2 us
  transfers between devices with their start and end apart: 11, of which 5 were waited for; matrix products, arithmetic and copies ran while one was open for 19% of the time, Pallas kernels for 0%

commit v1 on v0

--- a/solution.py
+++ b/solution.py
@@ -1,3 +1,4 @@
+import functools
 import jax
 import jax.numpy as jnp
 from jax import lax
@@ -5,6 +6,17 @@
 
 HD = 128
 TILE = 384
+
+
+def points_answer(z, ax_name):
+    block_next = lax.all_to_all(
+        jnp.stack(jnp.split(z, lax.axis_size(ax_name), axis=1)), ax_name, 0, 0
+    )
+    carry = jnp.concatenate(block_next, axis=0)
+    return carry
+
+
+obtain_the_shelves = functools.partial(points_answer, ax_name="seq")
 
 
 def extended_2(block, sides, width):
@@ -35,7 +47,7 @@
     q_heads, k_heads, v_heads = (
         lax.all_to_all(query, "seq", split_axis=1, concat_axis=0, tiled=True),
         lax.all_to_all(key_in, "seq", split_axis=1, concat_axis=0, tiled=True),
-        lax.all_to_all(value, "seq", split_axis=1, concat_axis=0, tiled=True),
+        obtain_the_shelves(value),
     )
     slab_rows = q_heads.shape[0]
     width_local = q_heads.shape[1]

time: 532 us -> 531 us (level)
  local copies, waits for them, and re-layouts: 141 us -> 151 us
  waiting for transfers between devices: 132 us -> 124 us
    unnamed x15 -> x22, local copies, waits for them, and re-layouts: 4.21 us -> 14.9 us
  transfers between devices with their start and end apart: 11 -> 11, of which waited for: 5 -> 5; matrix products, arithmetic and copies ran while one was open for 19% -> 21% of each run, Pallas kernels for 0% -> 0%
where the time goes in v1:
time: 531 us; the launch traced here: 523 us
  local copies, waits for them, and re-layouts  151 us (28%)
  waiting for transfers between devices  124 us (23%)
  matrix products  82.6 us (16%)
  other arithmetic  56.4 us (11%)
  blocking collectives  48.9 us (9%)
  starting transfers between devices  44.2 us (8%)
  between operations  14.5 us (3%)
    all_to_all x1, waiting for transfers between devices, body(): lax.all_to_all(query, 'seq', split_axis=1, concat_axis=0, tiled=True)  59.5 us
    all_to_all x1, blocking collectives, body(): lax.all_to_all(key_in, 'seq', split_axis=1, concat_axis=0, tiled=True)  31.4 us
    all_to_all x1, waiting for transfers between devices, body(): lax.all_to_all(attn_heads, 'seq', split_axis=0, concat_axis=1, tiled=True)  31.1 us
    dynamic_update_slice x9, local copies, waits for them, and re-layouts, body(): lax.map(backward_tile, (query_tiles, local_ids, saved_weights, grad_tiles))  30.4 us
    all_to_all x1, waiting for transfers between devices, points_answer(): lax.all_to_all(jnp.stack(jnp.split(z, lax.axis_size(ax_name), axis=1)), a...  24.8 us
    dynamic_update_slice x3, other arithmetic, body(): lax.map(forward_tile, (query_tiles, local_ids, window_count))  19.3 us
    all_to_all x1, blocking collectives, body(): lax.all_to_all(key_heads, 'seq', split_axis=0, concat_axis=1, tiled=True)  17.5 us
    convert_element_type x3, other arithmetic, backward_tile(): (weights * (grad_weights - centre) * factor).astype(jnp.bfloat16)  16.2 us
  transfers between devices with their start and end apart: 11, of which 5 were waited for; matrix products, arithmetic and copies ran while one was open for 21% of the time, Pallas kernels for 0%

profile of v1, /device:TPU:32, one launch (start us, length us, event | category | flops | bytes accessed | tf_op | source)
XLA Modules:
  0.0 522.7 jit_solution(4604646354567845550)
XLA Ops:
  20.1 10.0 %all-to-all-start.1 = ((bf16[8,144,256]{2,1,0:T(8,128)(2,1)}), bf16[8,144,256]{2,1,0:T(8,128)(2,1)S(1)}, u32[]{:S(2)}, u32[]{:S(2)}) async-start(bf16[8,144,256]{2,1,0:T(8,128)(2,1)} %bitcast_dynamic-update-slice_fusion.1), calls=%async_computation.1 | async-start | bytes 1179648 | tf_op jit(solution)/shard_map/all_to_all | solution.py:12
  31.3 24.8 %all-to-all-done.1 = bf16[8,144,256]{2,1,0:T(8,128)(2,1)S(1)} async-done(((bf16[8,144,256]{2,1,0:T(8,128)(2,1)}), bf16[8,144,256]{2,1,0:T(8,128)(2,1)S(1)}, u32[]{:S(2)}, u32[]{:S(2)}) %all-to-all-start.1) | async-done | bytes 589856 | tf_op jit(solution)/shard_map/all_to_all | solution.py:12
  56.1 31.4 %all_to_all.132 = bf16[144,8,256]{2,0,1:T(8,128)(2,1)S(1)} all-to-all(bf16[144,8,256]{2,0,1:T(8,128)(2,1)S(1)} %bitcast.220), channel_id=1, replica_groups=mesh['dp'=32,'seq'=8] {'seq'}, dimensions={1} | all-to-all | bytes 1179648 | tf_op jit(solution)/shard_map/all_to_all | solution.py:49
  93.8 3.5 all-to-all-start.2
  98.0 59.5 %all-to-all-done.2 = bf16[144,8,256]{2,0,1:T(8,128)(2,1)S(1)} async-done(((bf16[144,8,256]{2,0,1:T(8,128)(2,1)}), bf16[144,8,256]{2,0,1:T(8,128)(2,1)S(1)}, u32[]{:S(2)}, u32[]{:S(2)}) %all-to-all-start.2) | async-done | bytes 589856 | tf_op jit(solution)/shard_map/all_to_all | solution.py:48
  157.6 3.5 pad_maximum_fusion
  161.2 8.4 %reshape.124 = bf16[9,384,2,2,128]{4,3,2,1,0:T(2,128)(2,1)} reshape(bf16[3456,512]{1,0:T(8,128)(2,1)} %pad_maximum_fusion) | data formatting | bytes 7077888 | tf_op jit(solution)/shard_map/reshape | solution.py:57
  169.5 4.6 copy.102
  174.1 8.9 %convolution_convert_fusion.1 = bf16[144,2048]{1,0:T(8,128)(2,1)S(1)} fusion(bf16[144,3072]{1,0:T(8,128)(2,1)S(1)} %copy-done, bf16[2048,3072]{1,0:T(8,128)(2,1)} %all-gather.2.cloned.1.call-done), kind=kOutput, calls=%fused_computation.55 | convolution fusion | flops 1812234240 | bytes 14057472 | tf_op jit(solution)/shard_map/td,rd->tr/dot_general | solution.py:37
  183.8 4.7 all-to-all-start.4
  189.6 64.0 %while.26 = (s32[]{:T(128)}, bf16[3,384,2,128]{3,2,1,0:T(2,128)(2,1)}, f32[3,2,384,5,384]{2,4,3,1,0:T(8,128)}, s32[3,5]{1,0:T(4,128)S(1)}, bf16[9,384,2,2,128]{4...) while((s32[]{:T(128)}, bf16[3,384,2,128]{3,2,1,0:T(2,128)(2,1)}, ...), condition=%wide.region_3.4_spmd, body=%wide.region_0.3_spmd.sunk | while | flops 778665472 | bytes 66479360 | solution.py:85
  204.5 6.5 %bitcast_dynamic-update-slice_fusion.10 = f32[3,2,384,5,384]{2,4,3,1,0:T(8,128)} fusion(f32[3,2,384,5,384]{2,4,3,1,0:T(8,128)} %get-tuple-element.341, s32[]{:T(128)S(6)} %copy.212, f32[2,384]{1,0:T(2,128)S(1)} %fusion.72, f32[2,384]{1,0:T(2,128)S(1)} %get-tuple-element.315, f32[2,384,5,384]{1,3,2,0:T(8,128)} %copy-done.2, ...), kind=kLoop, calls=%fused_computation.2.clone.1 | loop fusion | flops 5898240 | bytes 11802633 | tf_op jit(solution)/shard_map/while/body/jit(dynamic_update_index_in_dim)/dynamic_update_slice | solution.py:85
  225.9 6.4 %bitcast_dynamic-update-slice_fusion.10 = f32[3,2,384,5,384]{2,4,3,1,0:T(8,128)} fusion(f32[3,2,384,5,384]{2,4,3,1,0:T(8,128)} %get-tuple-element.341, s32[]{:T(128)S(6)} %copy.212, f32[2,384]{1,0:T(2,128)S(1)} %fusion.72, f32[2,384]{1,0:T(2,128)S(1)} %get-tuple-element.315, f32[2,384,5,384]{1,3,2,0:T(8,128)} %copy-done.2, ...), kind=kLoop, calls=%fused_computation.2.clone.1 | loop fusion | flops 5898240 | bytes 11802633 | tf_op jit(solution)/shard_map/while/body/jit(dynamic_update_index_in_dim)/dynamic_update_slice | solution.py:85
  247.2 6.4 %bitcast_dynamic-update-slice_fusion.10 = f32[3,2,384,5,384]{2,4,3,1,0:T(8,128)} fusion(f32[3,2,384,5,384]{2,4,3,1,0:T(8,128)} %get-tuple-element.341, s32[]{:T(128)S(6)} %copy.212, f32[2,384]{1,0:T(2,128)S(1)} %fusion.72, f32[2,384]{1,0:T(2,128)S(1)} %get-tuple-element.315, f32[2,384,5,384]{1,3,2,0:T(8,128)} %copy-done.2, ...), kind=kLoop, calls=%fused_computation.2.clone.1 | loop fusion | flops 5898240 | bytes 11802633 | tf_op jit(solution)/shard_map/while/body/jit(dynamic_update_index_in_dim)/dynamic_update_slice | solution.py:85
  256.6 104.2 %while.27 = (s32[]{:T(128)}, bf16[3,384,2,128]{3,2,1,0:T(2,128)(2,1)}, f32[3,5,384,2,128]{4,3,2,1,0:T(2,128)}, f32[3,5,384,2,128]{4,3,2,1,0:T(2,128)}, s32[3,5]{...) while((s32[]{:T(128)}, ...), condition=%wide.region_6.7_spmd, body=%wide.region_4.6_spmd.sunk | while | flops 1518895360 | bytes 78260528 | solution.py:119
  256.8 3.1 gather_fusion.1
  261.1 3.7 fusion.80
  264.8 5.4 %fusion.81 = bf16[2,384,5,384]{1,3,2,0:T(8,128)(2,1)} fusion(f32[2,384,5,384]{1,3,2,0:T(8,128)S(1)} %get-tuple-element.326, f32[3,2,384,5,384]{2,4,3,1,0:T(8,128)} %get-tuple-element.381, s32[]{:T(128)S(6)} %copy.222, f32[2,384]{1,0:T(2,128)S(1)} %get-tuple-element.327), kind=kLoop, calls=%fused_computation.30.clone.1 | loop fusion | flops 5898240 | bytes 14748676 | tf_op jit(solution)/shard_map/while/body/eval_jaxpr/convert_element_type | solution.py:107
  274.4 3.7 fusion.83
  287.1 4.3 constant_dynamic-update-slice_fusion.11
  291.4 3.1 gather_fusion.1
  295.8 3.7 fusion.80
  299.5 5.4 %fusion.81 = bf16[2,384,5,384]{1,3,2,0:T(8,128)(2,1)} fusion(f32[2,384,5,384]{1,3,2,0:T(8,128)S(1)} %get-tuple-element.326, f32[3,2,384,5,384]{2,4,3,1,0:T(8,128)} %get-tuple-element.381, s32[]{:T(128)S(6)} %copy.222, f32[2,384]{1,0:T(2,128)S(1)} %get-tuple-element.327), kind=kLoop, calls=%fused_computation.30.clone.1 | loop fusion | flops 5898240 | bytes 14748676 | tf_op jit(solution)/shard_map/while/body/eval_jaxpr/convert_element_type | solution.py:107
  309.1 3.7 fusion.83
  321.7 4.4 constant_dynamic-update-slice_fusion.11
  326.1 3.1 gather_fusion.1
  330.5 3.7 fusion.80
  334.2 5.4 %fusion.81 = bf16[2,384,5,384]{1,3,2,0:T(8,128)(2,1)} fusion(f32[2,384,5,384]{1,3,2,0:T(8,128)S(1)} %get-tuple-element.326, f32[3,2,384,5,384]{2,4,3,1,0:T(8,128)} %get-tuple-element.381, s32[]{:T(128)S(6)} %copy.222, f32[2,384]{1,0:T(2,128)S(1)} %get-tuple-element.327), kind=kLoop, calls=%fused_computation.30.clone.1 | loop fusion | flops 5898240 | bytes 14748676 | tf_op jit(solution)/shard_map/while/body/eval_jaxpr/convert_element_type | solution.py:107
  343.8 3.7 fusion.83
  356.4 4.3 constant_dynamic-update-slice_fusion.11
  360.8 8.6 %reshape.127 = f32[15,98304]{1,0:T(8,128)} reshape(f32[3,5,384,2,128]{4,3,2,1,0:T(2,128)} %get-tuple-element.94) | data formatting | bytes 11796480 | tf_op jit(solution)/shard_map/reshape | solution.py:129
  369.3 8.1 %fusion.35 = f32[9,98304]{1,0:T(8,128)} fusion(f32[15,98304]{1,0:T(8,128)} %reshape.127, s32[15]{0:T(128)S(1)} %copy-done.8), kind=kOutput, calls=%fused_computation.78 | convolution fusion | flops 159252608 | bytes 9437244 | tf_op jit(solution)/shard_map/ns,nx->sx/dot_general | solution.py:126
  377.5 4.3 reshape.128
  381.8 4.2 constant_dynamic-update-slice_fusion.5
  386.0 8.5 %reshape.129 = f32[15,98304]{1,0:T(8,128)} reshape(f32[3,5,384,2,128]{4,3,2,1,0:T(2,128)} %get-tuple-element.95) | data formatting | bytes 11796480 | tf_op jit(solution)/shard_map/reshape | solution.py:135
  394.4 8.1 %fusion.34 = f32[9,98304]{1,0:T(8,128)} fusion(f32[15,98304]{1,0:T(8,128)} %reshape.129, s32[15]{0:T(128)S(1)} %copy-done.8), kind=kOutput, calls=%fused_computation.77 | convolution fusion | flops 159252608 | bytes 9437244 | tf_op jit(solution)/shard_map/ns,nx->sx/dot_general | solution.py:132
  402.6 4.1 reshape.130
  406.7 4.1 constant_dynamic-update-slice_fusion.4
  410.8 3.5 convert.10
  420.0 9.6 %all-to-all-start.3 = ((bf16[8,144,256]{2,1,0:T(8,128)(2,1)}), bf16[8,144,256]{2,1,0:T(8,128)(2,1)S(1)}, u32[]{:S(2)}, u32[]{:S(2)}) async-start(bf16[8,144,256]{2,1,0:T(8,128)(2,1)} %all_to_all.105), calls=%async_computation.3 | async-start | bytes 1179648 | tf_op jit(solution)/shard_map/all_to_all | solution.py:89
  432.3 31.1 %all-to-all-done.3 = bf16[8,144,256]{2,1,0:T(8,128)(2,1)S(1)} async-done(((bf16[8,144,256]{2,1,0:T(8,128)(2,1)}), bf16[8,144,256]{2,1,0:T(8,128)(2,1)S(1)}, u32[]{:S(2)}, u32[]{:S(2)}) %all-to-all-start.3) | async-done | bytes 589856 | tf_op jit(solution)/shard_map/all_to_all | solution.py:89
  463.4 4.2 all-to-all-start.5
  467.6 6.8 %fusion.33 = bf16[1152,512]{1,0:T(8,128)(2,1)S(1)} fusion(f32[3456,512]{1,0:T(8,128)} %constant_dynamic-update-slice_fusion.4, bf16[1152,512]{1,0:T(8,128)(2,1)} %collective-permute-done.3, bf16[1152,512]{1,0:T(8,128)(2,1)S(1)} %get-tuple-element.209, bf16[1152,512]{1,0:T(8,128)(2,1)S(1)} %get-tuple-element.210, bf16[1152,512]{1,0:T(8,128)(2,1)} %collective-permute-done.2), kind=kLoop, calls=%fused_computation.58 | loop fusion | flops 11206656 | bytes 8257536 | tf_op jit(solution)/shard_map/convert.1
  475.3 4.9 all-to-all-done.5
  480.2 17.5 %all_to_all.133 = bf16[8,144,256]{2,1,0:T(8,128)(2,1)S(1)} all-to-all(bf16[8,144,256]{2,1,0:T(8,128)(2,1)S(1)} %bitcast.221), channel_id=1, replica_groups=mesh['dp'=32,'seq'=8] {'seq'}, dimensions={0} | all-to-all | bytes 1179648 | tf_op jit(solution)/shard_map/all_to_all | solution.py:149
  497.7 3.5 all-to-all-start.7
  501.3 7.6 %convolution_convert_fusion = bf16[144,3072]{1,0:T(8,128)(2,1)} fusion(bf16[144,2048]{1,0:T(8,128)(2,1)S(1)} %bitcast.215, bf16[2048,3072]{1,0:T(8,128)(2,1)} %all-gather.2.cloned.1.call-done), kind=kOutput, calls=%fused_computation.53 | convolution fusion | flops 1812381696 | bytes 14057472 | tf_op jit(solution)/shard_map/dot_general | solution.py:36
  511.7 3.0 all-to-all-done.7
  (157 shorter events, 126.5 us)
Async XLA Ops:
  7.2 166.9 %copy-start = (bf16[144,3072]{1,0:T(8,128)(2,1)S(1)}, bf16[144,3072]{1,0:T(8,128)(2,1)}, u32[]{:S(2)}) copy-start(bf16[144,3072]{1,0:T(8,128)(2,1)} %param.15) | copy-start | bytes 2654212
  7.2 85.8 %copy-start.7 = (bf16[144,2048]{1,0:T(8,128)(2,1)S(1)}, bf16[144,2048]{1,0:T(8,128)(2,1)}, u32[]{:S(2)}) copy-start(bf16[144,2048]{1,0:T(8,128)(2,1)} %param.11) | copy-start | bytes 1769476
  7.2 90.2 %copy-start.9 = (s32[3,5]{1,0:T(4,128)S(1)}, s32[3,5]{1,0:T(4,128)}, u32[]{:S(2)}) copy-start(s32[3,5]{1,0:T(4,128)} %param.16) | copy-start | bytes 184
  7.2 166.9 %all-gather.2.cloned.1.call-start = ((), (), s32[]{:S(2)}) async-start(), calls=%async_computation.8 | async-start | bytes 12976128 | tf_op jit(solution)/shard_map/all_gather | solution.py:91
  20.1 36.0 %all-to-all-start.1 = ((bf16[8,144,256]{2,1,0:T(8,128)(2,1)}), bf16[8,144,256]{2,1,0:T(8,128)(2,1)S(1)}, u32[]{:S(2)}, u32[]{:S(2)}) async-start(bf16[8,144,256]{2,1,0:T(8,128)(2,1)} %bitcast_dynamic-update-slice_fusion.1), calls=%async_computation.1 | async-start | bytes 1179648 | tf_op jit(solution)/shard_map/all_to_all | solution.py:12
  88.6 69.0 %collective-permute-start.1 = (bf16[1152,512]{1,0:T(8,128)(2,1)}, bf16[1152,512]{1,0:T(8,128)(2,1)}, u32[]{:S(2)}, u32[]{:S(2)}) collective-permute-start(bf16[1152,512]{1,0:T(8,128)(2,1)} %pad_maximum_fusion.4), channel_id=1, source_target_pairs={{8,0},{16,8},{24,16},{32,24},{40,32},{48,40},{56,48},{64,56},{72,6... | collective-permute-start | bytes 3538952 | tf_op jit(solution)/shard_map/ppermute | solution.py:30
  90.5 67.1 %collective-permute-start = (bf16[1152,512]{1,0:T(8,128)(2,1)}, bf16[1152,512]{1,0:T(8,128)(2,1)}, u32[]{:S(2)}, u32[]{:S(2)}) collective-permute-start(bf16[1152,512]{1,0:T(8,128)(2,1)} %pad_maximum_fusion.4), channel_id=1, source_target_pairs={{0,8},{8,16},{16,24},{24,32},{32,40},{40,48},{48,56},{56,64},{64,7... | collective-permute-start | bytes 3538952 | tf_op jit(solution)/shard_map/ppermute | solution.py:27
  93.8 63.7 %all-to-all-start.2 = ((bf16[144,8,256]{2,0,1:T(8,128)(2,1)}), bf16[144,8,256]{2,0,1:T(8,128)(2,1)S(1)}, u32[]{:S(2)}, u32[]{:S(2)}) async-start(bf16[144,8,256]{2,0,1:T(8,128)(2,1)} %bitcast.159), calls=%async_computation.2 | async-start | bytes 1179648 | tf_op jit(solution)/shard_map/all_to_all | solution.py:48
  174.1 15.5 %copy-start.10 = (s32[3]{0:T(128)S(1)}, s32[3]{0:T(128)}, u32[]{:S(2)}) copy-start(s32[3]{0:T(128)} %param.17) | copy-start | bytes 40
  183.8 69.8 %all-to-all-start.4 = ((bf16[144,8,256]{2,0,1:T(8,128)(2,1)}), bf16[144,8,256]{2,0,1:T(8,128)(2,1)}, u32[]{:S(2)}, u32[]{:S(2)}) async-start(bf16[144,8,256]{2,0,1:T(8,128)(2,1)} %bitcast.158), calls=%async_computation.4 | async-start | bytes 1179648 | tf_op jit(solution)/shard_map/all_to_all | solution.py:94
  199.3 2.5 copy-start.2
  220.7 2.5 copy-start.2
  242.0 2.5 copy-start.2
  256.7 8.1 %copy-start.4 = (bf16[3,384,2,128]{3,2,1,0:T(2,128)(2,1)}, bf16[3,384,2,128]{3,2,1,0:T(2,128)(2,1)S(1)}, u32[]{:S(2)}) copy-start(bf16[3,384,2,128]{3,2,1,0:T(2,128)(2,1)S(1)} %get-tuple-element.382) | copy-start | bytes 1769476 | tf_op jit(solution)/shard_map/while
  264.8 5.4 %copy-start.3 = (bf16[5,384,1,2,128]{4,1,3,2,0:T(8,128)(2,1)S(1)}, bf16[5,384,1,2,128]{4,1,3,2,0:T(8,128)(2,1)}, u32[]{:S(2)}) copy-start(bf16[5,384,1,2,128]{4,1,3,2,0:T(8,128)(2,1)} %get-tuple-element.328) | copy-start | bytes 2949124 | tf_op jit(solution)/shard_map/while
  284.2 7.2 %copy-start.5 = (bf16[3,384,2,128]{3,2,1,0:T(2,128)(2,1)S(1)}, bf16[3,384,2,128]{3,2,1,0:T(2,128)(2,1)}, u32[]{:S(2)}) copy-start(bf16[3,384,2,128]{3,2,1,0:T(2,128)(2,1)} %copy-done.4) | copy-start | bytes 1769476 | tf_op jit(solution)/shard_map/while
  291.4 8.1 %copy-start.4 = (bf16[3,384,2,128]{3,2,1,0:T(2,128)(2,1)}, bf16[3,384,2,128]{3,2,1,0:T(2,128)(2,1)S(1)}, u32[]{:S(2)}) copy-start(bf16[3,384,2,128]{3,2,1,0:T(2,128)(2,1)S(1)} %get-tuple-element.382) | copy-start | bytes 1769476 | tf_op jit(solution)/shard_map/while
  299.5 5.4 %copy-start.3 = (bf16[5,384,1,2,128]{4,1,3,2,0:T(8,128)(2,1)S(1)}, bf16[5,384,1,2,128]{4,1,3,2,0:T(8,128)(2,1)}, u32[]{:S(2)}) copy-start(bf16[5,384,1,2,128]{4,1,3,2,0:T(8,128)(2,1)} %get-tuple-element.328) | copy-start | bytes 2949124 | tf_op jit(solution)/shard_map/while
  318.8 7.3 %copy-start.5 = (bf16[3,384,2,128]{3,2,1,0:T(2,128)(2,1)S(1)}, bf16[3,384,2,128]{3,2,1,0:T(2,128)(2,1)}, u32[]{:S(2)}) copy-start(bf16[3,384,2,128]{3,2,1,0:T(2,128)(2,1)} %copy-done.4) | copy-start | bytes 1769476 | tf_op jit(solution)/shard_map/while
  326.1 8.1 %copy-start.4 = (bf16[3,384,2,128]{3,2,1,0:T(2,128)(2,1)}, bf16[3,384,2,128]{3,2,1,0:T(2,128)(2,1)S(1)}, u32[]{:S(2)}) copy-start(bf16[3,384,2,128]{3,2,1,0:T(2,128)(2,1)S(1)} %get-tuple-element.382) | copy-start | bytes 1769476 | tf_op jit(solution)/shard_map/while
  334.2 5.4 %copy-start.3 = (bf16[5,384,1,2,128]{4,1,3,2,0:T(8,128)(2,1)S(1)}, bf16[5,384,1,2,128]{4,1,3,2,0:T(8,128)(2,1)}, u32[]{:S(2)}) copy-start(bf16[5,384,1,2,128]{4,1,3,2,0:T(8,128)(2,1)} %get-tuple-element.328) | copy-start | bytes 2949124 | tf_op jit(solution)/shard_map/while
  353.5 7.3 %copy-start.5 = (bf16[3,384,2,128]{3,2,1,0:T(2,128)(2,1)S(1)}, bf16[3,384,2,128]{3,2,1,0:T(2,128)(2,1)}, u32[]{:S(2)}) copy-start(bf16[3,384,2,128]{3,2,1,0:T(2,128)(2,1)} %copy-done.4) | copy-start | bytes 1769476 | tf_op jit(solution)/shard_map/while
  360.8 8.6 %copy-start.8 = (s32[15]{0:T(128)S(1)}, s32[15]{0:T(128)}, u32[]{:S(2)}) copy-start(s32[15]{0:T(128)} %eq.15) | copy-start | bytes 184
  410.8 8.0 %copy-start.6 = (bf16[3,384,2,128]{3,2,1,0:T(2,128)(2,1)S(1)}, bf16[3,384,2,128]{3,2,1,0:T(2,128)(2,1)}, u32[]{:S(2)}) copy-start(bf16[3,384,2,128]{3,2,1,0:T(2,128)(2,1)} %get-tuple-element.91) | copy-start | bytes 1769476
  414.5 53.2 %collective-permute-start.3 = (bf16[1152,512]{1,0:T(8,128)(2,1)S(1)}, bf16[1152,512]{1,0:T(8,128)(2,1)}, u32[]{:S(2)}, u32[]{:S(2)}) collective-permute-start(bf16[1152,512]{1,0:T(8,128)(2,1)S(1)} %get-tuple-element.210), channel_id=1, source_target_pairs={{8,0},{16,8},{24,16},{32,24},{40,32},{48,40},{56,48},{64,56},{72,6... | collective-permute-start | bytes 3538952 | tf_op jit(solution)/shard_map/ppermute | solution.py:30
  416.4 51.3 %collective-permute-start.2 = (bf16[1152,512]{1,0:T(8,128)(2,1)S(1)}, bf16[1152,512]{1,0:T(8,128)(2,1)}, u32[]{:S(2)}, u32[]{:S(2)}) collective-permute-start(bf16[1152,512]{1,0:T(8,128)(2,1)S(1)} %get-tuple-element.209), channel_id=1, source_target_pairs={{0,8},{8,16},{16,24},{24,32},{32,40},{40,48},{48,56},{56,64},{64,7... | collective-permute-start | bytes 3538952 | tf_op jit(solution)/shard_map/ppermute | solution.py:27
  420.0 43.4 %all-to-all-start.3 = ((bf16[8,144,256]{2,1,0:T(8,128)(2,1)}), bf16[8,144,256]{2,1,0:T(8,128)(2,1)S(1)}, u32[]{:S(2)}, u32[]{:S(2)}) async-start(bf16[8,144,256]{2,1,0:T(8,128)(2,1)} %all_to_all.105), calls=%async_computation.3 | async-start | bytes 1179648 | tf_op jit(solution)/shard_map/all_to_all | solution.py:89
  463.4 16.8 %all-to-all-start.5 = ((bf16[8,144,256]{2,1,0:T(8,128)(2,1)}), bf16[8,144,256]{2,1,0:T(8,128)(2,1)}, u32[]{:S(2)}, u32[]{:S(2)}) async-start(bf16[8,144,256]{2,1,0:T(8,128)(2,1)} %all_to_all.112), calls=%async_computation.5 | async-start | bytes 1179648 | tf_op jit(solution)/shard_map/all_to_all | solution.py:148
  497.7 17.1 %all-to-all-start.7 = ((bf16[8,144,256]{2,1,0:T(8,128)(2,1)}), bf16[8,144,256]{2,1,0:T(8,128)(2,1)S(1)}, u32[]{:S(2)}, u32[]{:S(2)}) async-start(bf16[8,144,256]{2,1,0:T(8,128)(2,1)} %bitcast.50), calls=%async_computation.7 | async-start | bytes 1179648 | tf_op jit(solution)/shard_map/all_to_all | solution.py:150
  501.3 14.3 %copy-start.1 = (bf16[144,3072]{1,0:T(8,128)(2,1)S(1)}, bf16[144,3072]{1,0:T(8,128)(2,1)}, u32[]{:S(2)}) copy-start(bf16[144,3072]{1,0:T(8,128)(2,1)} %param.15) | copy-start | bytes 2654212
Sparse Core Ops, SparseCore 0:
  9.9 132.3 all-gather.1
